TPU v7x, 32 devices: a whole 2x2x4 slice. The times are simulated.
32 devices in a mesh: clip: 2 (over y), height: 4 (over z), head: 4 (over x, core).
Axes of the slice: x: 2, y: 2, z: 4, core: 2. Of those that a mesh axis runs over, the one named last changes fastest.
Arguments:
- tokens: bfloat16 [8, 192, 5120], P(('clip', 'height'), None, 'head'), parts along dimension 0, may hold values from -6 to 6
- in_sign: int32 [5120], replicated, may hold values from 0 to 1
- qkv_codes: int32 [640, 3, 3072], P(None, None, 'head'), may hold values from 0 to 65535
- qkv_scale: float32 [3, 3072], P(None, 'head'), may hold values from 0.3 to 3
- qkv_sign: int32 [3, 3072], P(None, 'head'), may hold values from 0 to 1
- windows: int32 [8, 3, 27], P(('clip', 'height')), parts along dimension 0, may hold values from 0 to 11, as said below
- oin_sign: int32 [3072], P('head'), may hold values from 0 to 1
- out_codes: int32 [384, 5120], P('head'), may hold values from 0 to 65535
- out_scale: float32 [5120], replicated, may hold values from 2 to 20
- out_sign: int32 [5120], replicated, may hold values from 0 to 1
Outputs:
- attention_out: bfloat16 [8, 192, 5120], P(('clip', 'height'), 'head'), parts along dimension 0
There are 2 independent parts, one for each index of `clip`. A program takes and returns all parts, laid end to end along the dimension named above; an argument that names none is the same for every part. Nothing has to cross between parts.
Inputs may be any that keep to these rules, and one draw needn't show every extreme that they name: `windows`: each row lists the query tile itself and 26 further entries, each one of the 27 tiles of the 3 x 3 x 3 block of tiles centred on the query tile (each of the three coordinates clipped into the grid of 1 x 4 x 3 tiles); entries may repeat and appear in any order.
All inputs are finite; a program needn't handle non-finite values.
Results may differ from a plain program's by a relative error of at most 0.015.
Values may be sent and summed in bfloat16 or wider, within the bound.
A program may use at most 128 MiB of HBM per device.

v0:
```python
import jax
import jax.numpy as jnp
import numpy as np
from jax import lax
from jax.sharding import PartitionSpec as P

D = 5120
HD = 128
HEADS = 24
HAD = 128
TILE = 64
epsilon = 1e-06


def from_behind(shard, axis, by):
    peers = lax.axis_size(axis)
    pairs = [(i, i + by) for i in range(peers) if 0 <= i + by < peers]
    return lax.ppermute(shard, axis, pairs)


def sylvester(order_size):
    matrix_now = np.ones((1, 1), np.float32)
    seed_pair = np.array([[1.0, 1.0], [1.0, -1.0]], np.float32)
    while matrix_now.shape[0] < order_size:
        matrix_now = np.kron(matrix_now, seed_pair)
    return matrix_now


def signed(sign_bits):
    return (2 * sign_bits - 1).astype(jnp.float32)


def plane_levels(packed, column_scale, fan_in):
    powers = np.array([4**k for k in range(8)], np.int32)
    powers = jnp.asarray(powers.reshape((8,) + (1,) * packed.ndim), jnp.int32)
    digits = packed[None] // powers % 4
    return ((digits.astype(jnp.float32) - 1.5) * (column_scale * fan_in ** (-0.5))).astype(
        jnp.bfloat16
    )


def plane_product(rows_in, planes):
    row_count, inner = rows_in.shape
    grouped = rows_in.reshape(row_count, inner // 8, 8)
    return jnp.einsum("nik,kic->nc", grouped, planes, preferred_element_type=jnp.float32)


def rotate_exact(matrix_in):
    row_count, columns = matrix_in.shape
    hadamard = jnp.asarray(sylvester(HAD), jnp.float32)
    grouped = matrix_in.reshape(row_count, columns // HAD, HAD)
    turned = jnp.einsum("rbi,ij->rbj", grouped, hadamard, precision=lax.Precision.HIGHEST)
    return turned.reshape(row_count, columns) * HAD ** (-0.5)


def rotate_narrow(matrix_in, sign_values):
    row_count, columns = matrix_in.shape
    flipped = matrix_in * sign_values.astype(jnp.bfloat16)
    hadamard = jnp.asarray(sylvester(HAD), jnp.bfloat16)
    grouped = flipped.reshape(row_count, columns // HAD, HAD)
    turned = jnp.einsum("rbi,ij->rbj", grouped, hadamard, preferred_element_type=jnp.float32)
    return (turned.reshape(row_count, columns) * HAD ** (-0.5)).astype(jnp.bfloat16)


def normalize(vectors):
    return vectors / jnp.sqrt(jnp.mean(vectors * vectors, axis=-1, keepdims=True) + epsilon)


def tile_allowed(listed, key_ids):
    tile_count = key_ids.shape[0]
    allowed = jnp.any(listed[:, :, None] == key_ids[None, None, :], axis=1)
    allowed = jnp.broadcast_to(allowed[:, None, :, None], (listed.shape[0], TILE, tile_count, TILE))
    return allowed.reshape(listed.shape[0] * TILE, tile_count * TILE)


def attend_block(queries, near_keys, near_values, allowed):
    score = jnp.einsum(
        "qhd,khd->hqk", queries, near_keys, preferred_element_type=jnp.float32
    ) * HD ** (-0.5)
    weight = jnp.where(allowed[None], jnp.exp(score), 0.0)
    totals = jnp.sum(weight, axis=-1)
    gathered_sum = jnp.einsum(
        "hqk,khd->qhd", weight.astype(jnp.bfloat16), near_values, preferred_element_type=jnp.float32
    )
    return (gathered_sum, totals)


def on_device(
    tokens,
    in_sign,
    qkv_codes,
    qkv_scale,
    qkv_sign,
    windows,
    oin_sign,
    out_codes,
    out_scale,
    out_sign,
):
    head_count = lax.axis_size("head")
    head_place = lax.axis_index("head")
    row_place = lax.axis_index("height")
    flat_tokens = tokens[0]
    row_count = flat_tokens.shape[0]
    qkv_planes = plane_levels(qkv_codes, qkv_scale, D)
    qkv_planes = qkv_planes.reshape(8, qkv_codes.shape[0], -1)
    whole_rows = lax.all_gather(flat_tokens, "head", axis=1, tiled=True)
    turned = rotate_narrow(whole_rows, signed(in_sign))
    projected = plane_product(turned, qkv_planes)
    local_heads = qkv_scale.shape[1] // HD
    mixed = rotate_exact(projected) * signed(qkv_sign).reshape(-1)
    mixed = mixed.reshape(row_count, 3, local_heads, HD)
    queries = normalize(mixed[:, 0]).astype(jnp.bfloat16)
    key_rows = normalize(mixed[:, 1]).astype(jnp.bfloat16)
    value_rows = mixed[:, 2].astype(jnp.bfloat16)
    key_value = jnp.stack([key_rows, value_rows])
    distances = (5, 4, 3, 1, -1, -3, -4, -5)
    neighbours = [from_behind(key_value, "height", offset) for offset in distances]
    listed = windows[0]
    qtile_count = listed.shape[0]
    tile_steps = jnp.arange(qtile_count, dtype=jnp.int32)
    own_ids = row_place * qtile_count + tile_steps
    near_ids = [(row_place - offset) * qtile_count + tile_steps for offset in distances]
    ordered = [key_value] + neighbours
    near_keys = jnp.concatenate([block[0] for block in ordered], 0)
    near_values = jnp.concatenate([block[1] for block in ordered], 0)
    all_ids = jnp.concatenate([own_ids] + near_ids, 0)
    gathered_sum, totals = attend_block(
        queries, near_keys, near_values, tile_allowed(listed, all_ids)
    )
    attended = (gathered_sum / totals.T[:, :, None]).astype(jnp.bfloat16)
    attended = attended.reshape(row_count, local_heads * HD)
    rotated_heads = rotate_narrow(attended, signed(oin_sign))
    out_planes = plane_levels(out_codes, out_scale, HEADS * HD)
    share_rows = row_count // head_count
    partial_rows = plane_product(rotated_heads, out_planes)
    summed = lax.psum(partial_rows.astype(jnp.bfloat16), "head").astype(jnp.float32)
    own_rows = lax.dynamic_slice_in_dim(summed, head_place * share_rows, share_rows, 0)
    result_rows = (rotate_exact(own_rows) * signed(out_sign)).astype(jnp.bfloat16)
    return result_rows[None]


def solution(mesh):
    return jax.shard_map(
        on_device,
        mesh=mesh,
        in_specs=(
            P(("clip", "height"), None, "head"),
            P(),
            P(None, None, "head"),
            P(None, "head"),
            P(None, "head"),
            P(("clip", "height"), None, None),
            P("head"),
            P("head", None),
            P(),
            P(),
        ),
        out_specs=P(("clip", "height"), "head", None),
        check_vma=False,
    )
```

profile of v0, /device:TPU:0, one launch (start us, length us, event | category | flops | bytes accessed | tf_op | source)
XLA Modules:
  0.0 894.5 jit_solution(4490852834834881463)
XLA Ops:
  6.5 0.0 all-gather.3.cloned.1.call-start
  6.5 0.7 all-gather.3.cloned.1.call-update
  7.3 0.0 all-reduce.2.cloned.1.call-start
  7.3 7.8 copy.24
  15.1 4.3 sign_compare_fusion
  19.4 0.0 copy-done.11
  19.4 0.0 copy-start.12
  19.4 0.0 copy-start.17
  19.4 0.0 copy-start.14
  19.5 0.0 copy-start.10
  19.5 0.0 copy-start.8
  19.5 0.0 copy-start
  19.5 490.1 %fusion.4 = bf16[18,128,640,8]{2,3,1,0:T(8,128)(2,1)} fusion(f32[18,128]{1,0:T(8,128)S(1)} %mul.173, s32[8]{0:T(128)S(1)} %copy-done.18, s32[18,128,640]{2,1,0:T(8,128)} %bitcast.138, pred[18,128,640]{2,1,0:T(8,128)(4,1)S(1)} %bitcast.142), kind=kLoop, calls=%fused_computation.8 | loop fusion | flops 247726080 | bytes 30975008 | tf_op jit(solution)/shard_map/convert_element_type | solution.py:37
  509.6 0.0 copy-done.12
  509.6 0.6 copy.39
  510.3 0.6 concatenate.10
  510.9 0.5 fusion.75
  511.4 0.6 broadcast_multiply_fusion.1
  512.0 1.3 sign_compare_fusion.1
  513.3 1.7 fusion.31
  515.0 0.0 copy-start.5
  515.0 0.3 copy.32
  515.4 0.4 copy-done.5
  515.8 2.5 multiply_convert_fusion
  518.3 3.8 copy.23
  522.1 3.4 copy.26
  525.5 15.8 %fusion.6 = f32[192,18,128,1]{2,0,3,1:T(8,128)S(1)} fusion(bf16[18,128,640,8]{2,3,1,0:T(8,128)(2,1)} %fusion.4, bf16[192,640,8]{1,0,2:T(8,128)(2,1)} %copy.26), kind=kOutput, calls=%fused_computation.11 | convolution fusion | flops 4529848320 | bytes 27328512 | tf_op jit(solution)/shard_map/nik,kic->nc/dot_general | solution.py:45
  541.3 1.6 fusion.32
  542.9 0.1 broadcast_multiply_fusion
  543.1 0.0 copy-start.13
  543.1 0.0 copy-start.16
  543.1 1.0 multiply_reduce_fusion
  544.1 0.2 fusion.51
  544.4 0.9 pad_maximum_fusion
  545.2 0.7 collective-permute-start
  546.0 0.1 compare_reduce_fusion
  546.1 0.3 broadcast_in_dim.12
  546.3 1.3 broadcast_in_dim.13
  547.7 7.3 collective-permute-start.1
  554.9 1.3 collective-permute-start.2
  556.3 1.3 collective-permute-start.3
  557.6 1.3 collective-permute-start.4
  558.9 1.0 fusion.54
  559.8 0.7 add_sqrt_fusion
  560.6 0.0 collective-permute-done
  560.7 8.3 collective-permute-done.1
  569.0 11.5 %collective-permute-done.2 = bf16[2,192,6,128]{3,1,2,0:T(8,128)(2,1)S(1)} collective-permute-done((bf16[2,192,6,128]{3,1,2,0:T(8,128)(2,1)}, bf16[2,192,6,128]{3,1,2,0:T(8,128)(2,1)S(1)}, u32[]{:S(2)}, u32[]{:S(2)}) %collective-permute-start.2) | collective-permute-done | bytes 589856 | tf_op jit(solution)/shard_map/ppermute | solution.py:18
  580.5 5.3 collective-permute-done.3
  585.8 0.0 collective-permute-done.4
  585.9 0.1 fusion.68
  586.0 5.0 fusion.17
  591.3 1.6 copy-done.7
  592.9 6.0 fusion.37
  598.9 0.2 copy.28
  599.1 0.0 copy-start.9
  599.1 237.7 %fusion.22 = bf16[192,5120]{1,0:T(8,128)(2,1)} fusion(f32[5120]{0:T(1024)} %broadcast_multiply_fusion.1, s32[8]{0:T(128)} %constant.118, s32[96,5120]{1,0:T(8,128)S(1)} %copy-done.1, pred[96,5120]{1,0:T(8,128)(4,1)S(1)} %copy-done.2, bf16[192,96,8]{0,2,1:T(8,128)(2,1)S(1)} %bitcast.144), kind=kOutput, calls=%fused_computation.30 | convolution fusion | flops 1593507840 | bytes 4739104 | tf_op jit(solution)/shard_map/nik,kic->nc/dot_general | solution.py:45
  836.8 0.0 all-reduce.2.cloned.1.call-update
  836.9 0.0 copy-done.9
  836.9 47.6 %all-reduce.2.cloned.1.call-done = bf16[192,5120]{1,0:T(8,128)(2,1)} async-done(((bf16[192,5120]{1,0:T(8,128)(2,1)}), bf16[192,5120]{1,0:T(8,128)(2,1)}) %all-reduce.2.cloned.1.call-update) | async-done | bytes 1966096 | tf_op jit(solution)/shard_map/psum | solution.py:137
  884.5 1.1 dynamic-slice_bitcast_fusion
  885.5 0.1 copy.33
  885.6 0.5 fusion.85
  886.1 0.2 reshape.147
  886.3 0.8 multiply_convert_fusion.1
  (51 shorter events, 0.7 us)
Async XLA Ops:
  6.5 506.8 %all-gather.3.cloned.1.call-start = ((), (), s32[]{:S(2)}) async-start(), calls=%async_computation.1 | async-start | bytes 2457600 | tf_op jit(solution)/shard_map/all_gather | solution.py:107
  7.3 877.2 %all-reduce.2.cloned.1.call-start = ((), (), s32[]{:S(2)}) async-start(), calls=%async_computation | async-start | bytes 3932160 | tf_op jit(solution)/shard_map/psum | solution.py:137
  15.1 4.3 copy-start.11
  15.1 4.3 copy-start.18
  19.4 490.1 %copy-start.12 = (s32[3,768]{1,0:T(4,128)S(1)}, s32[3,768]{1,0:T(4,128)}, u32[]{:S(2)}) copy-start(s32[3,768]{1,0:T(4,128)} %param.20) | copy-start | bytes 27652
  19.4 490.2 %copy-start.17 = (s32[1,3,27]{2,0,1:T(1,128)S(1)}, s32[1,3,27]{2,0,1:T(1,128)}, u32[]{:S(2)}) copy-start(s32[1,3,27]{2,0,1:T(1,128)} %param.21) | copy-start | bytes 976
  19.4 491.4 %copy-start.14 = (s32[768]{0:T(1024)S(1)}, s32[768]{0:T(1024)}, u32[]{:S(2)}) copy-start(s32[768]{0:T(1024)} %param.22) | copy-start | bytes 9220
  19.5 492.0 %copy-start.10 = (s32[5120]{0:T(1024)S(1)}, s32[5120]{0:T(1024)}, u32[]{:S(2)}) copy-start(s32[5120]{0:T(1024)} %param.17) | copy-start | bytes 61444
  19.5 492.0 %copy-start.8 = (f32[5120]{0:T(1024)S(1)}, f32[5120]{0:T(1024)}, u32[]{:S(2)}) copy-start(f32[5120]{0:T(1024)} %param.24) | copy-start | bytes 61444
  19.5 492.6 %copy-start = (s32[96,5120]{1,0:T(8,128)S(1)}, s32[96,5120]{1,0:T(8,128)}, u32[]{:S(2)}) copy-start(s32[96,5120]{1,0:T(8,128)} %param.23) | copy-start | bytes 5898244
  515.0 0.8 copy-start.5
  525.5 15.8 %copy-start.3 = (f32[128,128,1]{1,0,2:T(8,128)S(1)}, f32[128,128,1]{1,0,2:T(8,128)}, u32[]{:S(2)}) copy-start(f32[128,128,1]{1,0,2:T(8,128)} %constant.125) | copy-start | bytes 196612
  543.1 2.9 copy-start.13
  543.1 2.9 copy-start.16
  544.1 1.8 copy-start.4
  545.2 15.3 %collective-permute-start = (bf16[2,192,6,128]{3,1,2,0:T(8,128)(2,1)}, bf16[2,192,6,128]{3,1,2,0:T(8,128)(2,1)S(1)}, u32[]{:S(2)}, u32[]{:S(2)}) collective-permute-start(bf16[2,192,6,128]{3,1,2,0:T(8,128)(2,1)} %pad_maximum_fusion), channel_id=1, source_target_pairs={} | collective-permute-start | bytes 1769480 | tf_op jit(solution)/shard_map/ppermute | solution.py:18
  547.7 21.3 %collective-permute-start.1 = (bf16[2,192,6,128]{3,1,2,0:T(8,128)(2,1)}, bf16[2,192,6,128]{3,1,2,0:T(8,128)(2,1)S(1)}, u32[]{:S(2)}, u32[]{:S(2)}) collective-permute-start(bf16[2,192,6,128]{3,1,2,0:T(8,128)(2,1)} %pad_maximum_fusion), channel_id=1, source_target_pairs={{0,12},{1,13},{2,14},{3,15},{16,28},{17,29},{18,30},{19,31}} | collective-permute-start | bytes 1769480 | tf_op jit(solution)/shard_map/ppermute | solution.py:18
  554.9 25.5 %collective-permute-start.2 = (bf16[2,192,6,128]{3,1,2,0:T(8,128)(2,1)}, bf16[2,192,6,128]{3,1,2,0:T(8,128)(2,1)S(1)}, u32[]{:S(2)}, u32[]{:S(2)}) collective-permute-start(bf16[2,192,6,128]{3,1,2,0:T(8,128)(2,1)} %pad_maximum_fusion), channel_id=1, source_target_pairs={{0,4},{4,8},{8,12},{1,5},{5,9},{9,13},{2,6},{6,10},{10,14},{3,7},{... | collective-permute-start | bytes 1769480 | tf_op jit(solution)/shard_map/ppermute | solution.py:18
  556.3 29.5 %collective-permute-start.3 = (bf16[2,192,6,128]{3,1,2,0:T(8,128)(2,1)}, bf16[2,192,6,128]{3,1,2,0:T(8,128)(2,1)S(1)}, u32[]{:S(2)}, u32[]{:S(2)}) collective-permute-start(bf16[2,192,6,128]{3,1,2,0:T(8,128)(2,1)} %pad_maximum_fusion), channel_id=1, source_target_pairs={{4,0},{8,4},{12,8},{5,1},{9,5},{13,9},{6,2},{10,6},{14,10},{7,3},{... | collective-permute-start | bytes 1769480 | tf_op jit(solution)/shard_map/ppermute | solution.py:18
  557.6 28.2 %collective-permute-start.4 = (bf16[2,192,6,128]{3,1,2,0:T(8,128)(2,1)}, bf16[2,192,6,128]{3,1,2,0:T(8,128)(2,1)S(1)}, u32[]{:S(2)}, u32[]{:S(2)}) collective-permute-start(bf16[2,192,6,128]{3,1,2,0:T(8,128)(2,1)} %pad_maximum_fusion), channel_id=1, source_target_pairs={{12,0},{13,1},{14,2},{15,3},{28,16},{29,17},{30,18},{31,19}} | collective-permute-start | bytes 1769480 | tf_op jit(solution)/shard_map/ppermute | solution.py:18
  591.0 1.9 copy-start.6
  591.0 1.9 copy-start.15
  591.3 1.6 copy-start.7
  592.9 6.2 copy-start.1
  592.9 6.2 copy-start.2
  599.1 237.7 %copy-start.9 = (s32[5120]{0:T(1024)S(1)}, s32[5120]{0:T(1024)}, u32[]{:S(2)}) copy-start(s32[5120]{0:T(1024)} %param.25) | copy-start | bytes 61444
Sparse Core Ops, SparseCore 0:
  8.9 24.5 all-gather.2
  837.0 47.4 all-reduce.1
where the time goes:
time: 908 us; the launch traced here: 894 us
  other arithmetic  503 us (55%)
  matrix products  269 us (30%)
  waiting for transfers between devices  73.3 us (8%)
  local copies, waits for them, and re-layouts  22.3 us (2%)
  between operations  14.5 us (2%)
  starting transfers between devices  11.9 us (1%)
    convert_element_type x1, other arithmetic, plane_levels(): ((digits.astype(jnp.float32) - 1.5) * (column_scale * fan_in ** (-0.5)))....  490 us
    dot_general x2, matrix products, plane_product(): jnp.einsum('nik,kic->nc', grouped, planes, preferred_element_type=jnp.flo...  253 us
    psum x1, waiting for transfers between devices, on_device(): lax.psum(partial_rows.astype(jnp.bfloat16), 'head').astype(jnp.float32)  47.6 us
    ppermute x5, waiting for transfers between devices, from_behind(): return lax.ppermute(shard, axis, pairs)  25 us
  transfers between devices with their start and end apart: 7, of which 4 were waited for; matrix products, arithmetic and copies ran while one was open for 57% of the time, Pallas kernels for 0%

commit v1 on v0

--- a/solution.py
+++ b/solution.py
@@ -134,7 +134,9 @@
     out_planes = plane_levels(out_codes, out_scale, HEADS * HD)
     share_rows = row_count // head_count
     partial_rows = plane_product(rotated_heads, out_planes)
-    summed = lax.psum(partial_rows.astype(jnp.bfloat16), "head").astype(jnp.float32)
+    summed = jnp.sum(lax.all_gather(partial_rows.astype(jnp.bfloat16), "head"), axis=0).astype(
+        jnp.float32
+    )
     own_rows = lax.dynamic_slice_in_dim(summed, head_place * share_rows, share_rows, 0)
     result_rows = (rotate_exact(own_rows) * signed(out_sign)).astype(jnp.bfloat16)
     return result_rows[None]

time: 908 us -> 918 us (1.011)
    all_gather x0 -> x1, waiting for transfers between devices: none -> 53.6 us  [on_device(): lax.all_gather(partial_rows.astype(jnp.bfloat16), 'head')]
    psum x1 -> x0, waiting for transfers between devices: 47.6 us -> none  [on_device(): lax.psum(partial_rows.astype(jnp.bfloat16), 'head').astype(jnp.float32)]
  transfers between devices with their start and end apart: 7 -> 7, of which waited for: 4 -> 4; matrix products, arithmetic and copies ran while one was open for 57% -> 56% of each run, Pallas kernels for 0% -> 0%
where the time goes in v1:
time: 918 us; the launch traced here: 905 us
  other arithmetic  508 us (55%)
  matrix products  270 us (29%)
  waiting for transfers between devices  79.4 us (9%)
  local copies, waits for them, and re-layouts  21.3 us (2%)
  between operations  14.5 us (2%)
  starting transfers between devices  11.9 us (1%)
    convert_element_type x1, other arithmetic, plane_levels(): ((digits.astype(jnp.float32) - 1.5) * (column_scale * fan_in ** (-0.5)))....  490 us
    dot_general x2, matrix products, plane_product(): jnp.einsum('nik,kic->nc', grouped, planes, preferred_element_type=jnp.flo...  255 us
    all_gather x1, waiting for transfers between devices, on_device(): lax.all_gather(partial_rows.astype(jnp.bfloat16), 'head')  53.6 us
    ppermute x5, waiting for transfers between devices, from_behind(): return lax.ppermute(shard, axis, pairs)  25 us
  transfers between devices with their start and end apart: 7, of which 4 were waited for; matrix products, arithmetic and copies ran while one was open for 56% of the time, Pallas kernels for 0%

profile of v1, /device:TPU:0, one launch (start us, length us, event | category | flops | bytes accessed | tf_op | source)
XLA Modules:
  0.0 905.5 jit_solution(16786760657270790944)
XLA Ops:
  6.5 0.0 all-gather.5.cloned.1.call-start
  6.5 0.7 all-gather.5.cloned.1.call-update
  7.3 0.0 all-gather.7.cloned.1.call-start
  7.3 7.8 copy.24
  15.1 4.3 sign_compare_fusion
  19.4 0.0 copy-done.11
  19.4 0.0 copy-start.12
  19.4 0.0 copy-start.17
  19.4 0.0 copy-start.14
  19.5 0.0 copy-start.10
  19.5 0.0 copy-start.8
  19.5 0.0 copy-start
  19.5 490.1 %fusion.4 = bf16[18,128,640,8]{2,3,1,0:T(8,128)(2,1)} fusion(f32[18,128]{1,0:T(8,128)S(1)} %mul.173, s32[8]{0:T(128)S(1)} %copy-done.18, s32[18,128,640]{2,1,0:T(8,128)} %bitcast.139, pred[18,128,640]{2,1,0:T(8,128)(4,1)S(1)} %bitcast.144), kind=kLoop, calls=%fused_computation.8 | loop fusion | flops 247726080 | bytes 30975008 | tf_op jit(solution)/shard_map/convert_element_type | solution.py:37
  509.6 0.6 copy.39
  510.3 0.6 concatenate.10
  510.9 0.0 copy-done.14
  510.9 0.5 fusion.75
  511.4 0.6 broadcast_multiply_fusion.1
  512.0 1.3 sign_compare_fusion.1
  513.3 1.7 fusion.31
  515.0 0.0 copy-start.5
  515.0 0.3 copy.32
  515.4 0.4 copy-done.5
  515.8 2.5 multiply_convert_fusion
  518.3 3.8 copy.23
  522.1 3.4 copy.26
  525.5 15.8 %fusion.6 = f32[192,18,128,1]{2,0,3,1:T(8,128)S(1)} fusion(bf16[18,128,640,8]{2,3,1,0:T(8,128)(2,1)} %fusion.4, bf16[192,640,8]{1,0,2:T(8,128)(2,1)} %copy.26), kind=kOutput, calls=%fused_computation.11 | convolution fusion | flops 4529848320 | bytes 27328512 | tf_op jit(solution)/shard_map/nik,kic->nc/dot_general | solution.py:45
  541.3 1.6 fusion.32
  542.9 0.1 broadcast_multiply_fusion
  543.1 0.0 copy-start.13
  543.1 0.0 copy-start.16
  543.1 1.0 multiply_reduce_fusion
  544.1 0.2 fusion.51
  544.4 0.9 pad_maximum_fusion
  545.2 0.7 collective-permute-start
  546.0 0.1 compare_reduce_fusion
  546.1 0.3 broadcast_in_dim.12
  546.3 1.3 broadcast_in_dim.13
  547.7 7.3 collective-permute-start.1
  554.9 1.3 collective-permute-start.2
  556.3 1.3 collective-permute-start.3
  557.6 1.3 collective-permute-start.4
  558.9 1.0 fusion.54
  559.8 0.7 add_sqrt_fusion
  560.6 0.0 collective-permute-done
  560.7 8.3 collective-permute-done.1
  569.0 11.5 %collective-permute-done.2 = bf16[2,192,6,128]{3,1,2,0:T(8,128)(2,1)S(1)} collective-permute-done((bf16[2,192,6,128]{3,1,2,0:T(8,128)(2,1)}, bf16[2,192,6,128]{3,1,2,0:T(8,128)(2,1)S(1)}, u32[]{:S(2)}, u32[]{:S(2)}) %collective-permute-start.2) | collective-permute-done | bytes 589856 | tf_op jit(solution)/shard_map/ppermute | solution.py:18
  580.5 5.3 collective-permute-done.3
  585.8 0.0 collective-permute-done.4
  585.9 0.1 fusion.68
  586.0 5.0 fusion.17
  591.3 1.6 copy-done.7
  592.9 6.0 fusion.37
  598.9 0.2 copy.28
  599.1 0.0 copy-start.9
  599.1 238.8 %fusion.22 = bf16[192,5120]{1,0:T(8,128)(2,1)} fusion(f32[5120]{0:T(1024)} %broadcast_multiply_fusion.1, s32[8]{0:T(128)} %constant.120, s32[96,5120]{1,0:T(8,128)S(1)} %copy-done.1, pred[96,5120]{1,0:T(8,128)(4,1)S(1)} %copy-done.2, bf16[192,96,8]{0,2,1:T(8,128)(2,1)S(1)} %bitcast.146), kind=kOutput, calls=%fused_computation.30 | convolution fusion | flops 1593507840 | bytes 4739104 | tf_op jit(solution)/shard_map/nik,kic->nc/dot_general | solution.py:45
  837.9 0.0 all-gather.7.cloned.1.call-update
  837.9 0.0 copy-done.9
  838.0 53.6 %all-gather.7.cloned.1.call-done = bf16[768,5120]{1,0:T(8,128)(2,1)} async-done(((bf16[192,5120]{1,0:T(8,128)(2,1)}), bf16[768,5120]{1,0:T(8,128)(2,1)}) %all-gather.7.cloned.1.call-update) | async-done | bytes 7864336 | tf_op jit(solution)/shard_map/all_gather | solution.py:137
  891.6 4.8 reduce_sum.42
  896.5 0.1 copy.33
  896.6 0.5 fusion.85
  897.1 0.2 reshape.147
  897.3 0.8 multiply_convert_fusion.1
  (52 shorter events, 0.8 us)
Async XLA Ops:
  6.5 506.8 %all-gather.5.cloned.1.call-start = ((), (), s32[]{:S(2)}) async-start(), calls=%async_computation | async-start | bytes 2457600 | tf_op jit(solution)/shard_map/all_gather | solution.py:107
  7.3 884.3 %all-gather.7.cloned.1.call-start = ((), (), s32[]{:S(2)}) async-start(), calls=%async_computation.1 | async-start | bytes 9830400 | tf_op jit(solution)/shard_map/all_gather | solution.py:137
  15.1 4.3 copy-start.11
  15.1 4.3 copy-start.18
  19.4 490.1 %copy-start.12 = (s32[3,768]{1,0:T(4,128)S(1)}, s32[3,768]{1,0:T(4,128)}, u32[]{:S(2)}) copy-start(s32[3,768]{1,0:T(4,128)} %param.20) | copy-start | bytes 27652
  19.4 490.2 %copy-start.17 = (s32[1,3,27]{2,0,1:T(1,128)S(1)}, s32[1,3,27]{2,0,1:T(1,128)}, u32[]{:S(2)}) copy-start(s32[1,3,27]{2,0,1:T(1,128)} %param.21) | copy-start | bytes 976
  19.4 491.4 %copy-start.14 = (s32[768]{0:T(1024)S(1)}, s32[768]{0:T(1024)}, u32[]{:S(2)}) copy-start(s32[768]{0:T(1024)} %param.22) | copy-start | bytes 9220
  19.5 492.0 %copy-start.10 = (s32[5120]{0:T(1024)S(1)}, s32[5120]{0:T(1024)}, u32[]{:S(2)}) copy-start(s32[5120]{0:T(1024)} %param.17) | copy-start | bytes 61444
  19.5 492.0 %copy-start.8 = (f32[5120]{0:T(1024)S(1)}, f32[5120]{0:T(1024)}, u32[]{:S(2)}) copy-start(f32[5120]{0:T(1024)} %param.24) | copy-start | bytes 61444
  19.5 492.6 %copy-start = (s32[96,5120]{1,0:T(8,128)S(1)}, s32[96,5120]{1,0:T(8,128)}, u32[]{:S(2)}) copy-start(s32[96,5120]{1,0:T(8,128)} %param.23) | copy-start | bytes 5898244
  515.0 0.8 copy-start.5
  525.5 15.8 %copy-start.3 = (f32[128,128,1]{1,0,2:T(8,128)S(1)}, f32[128,128,1]{1,0,2:T(8,128)}, u32[]{:S(2)}) copy-start(f32[128,128,1]{1,0,2:T(8,128)} %constant.127) | copy-start | bytes 196612
  543.1 2.9 copy-start.13
  543.1 2.9 copy-start.16
  544.1 1.8 copy-start.4
  545.2 15.3 %collective-permute-start = (bf16[2,192,6,128]{3,1,2,0:T(8,128)(2,1)}, bf16[2,192,6,128]{3,1,2,0:T(8,128)(2,1)S(1)}, u32[]{:S(2)}, u32[]{:S(2)}) collective-permute-start(bf16[2,192,6,128]{3,1,2,0:T(8,128)(2,1)} %pad_maximum_fusion), channel_id=1, source_target_pairs={} | collective-permute-start | bytes 1769480 | tf_op jit(solution)/shard_map/ppermute | solution.py:18
  547.7 21.3 %collective-permute-start.1 = (bf16[2,192,6,128]{3,1,2,0:T(8,128)(2,1)}, bf16[2,192,6,128]{3,1,2,0:T(8,128)(2,1)S(1)}, u32[]{:S(2)}, u32[]{:S(2)}) collective-permute-start(bf16[2,192,6,128]{3,1,2,0:T(8,128)(2,1)} %pad_maximum_fusion), channel_id=1, source_target_pairs={{0,12},{1,13},{2,14},{3,15},{16,28},{17,29},{18,30},{19,31}} | collective-permute-start | bytes 1769480 | tf_op jit(solution)/shard_map/ppermute | solution.py:18
  554.9 25.5 %collective-permute-start.2 = (bf16[2,192,6,128]{3,1,2,0:T(8,128)(2,1)}, bf16[2,192,6,128]{3,1,2,0:T(8,128)(2,1)S(1)}, u32[]{:S(2)}, u32[]{:S(2)}) collective-permute-start(bf16[2,192,6,128]{3,1,2,0:T(8,128)(2,1)} %pad_maximum_fusion), channel_id=1, source_target_pairs={{0,4},{4,8},{8,12},{1,5},{5,9},{9,13},{2,6},{6,10},{10,14},{3,7},{... | collective-permute-start | bytes 1769480 | tf_op jit(solution)/shard_map/ppermute | solution.py:18
  556.3 29.5 %collective-permute-start.3 = (bf16[2,192,6,128]{3,1,2,0:T(8,128)(2,1)}, bf16[2,192,6,128]{3,1,2,0:T(8,128)(2,1)S(1)}, u32[]{:S(2)}, u32[]{:S(2)}) collective-permute-start(bf16[2,192,6,128]{3,1,2,0:T(8,128)(2,1)} %pad_maximum_fusion), channel_id=1, source_target_pairs={{4,0},{8,4},{12,8},{5,1},{9,5},{13,9},{6,2},{10,6},{14,10},{7,3},{... | collective-permute-start | bytes 1769480 | tf_op jit(solution)/shard_map/ppermute | solution.py:18
  557.6 28.2 %collective-permute-start.4 = (bf16[2,192,6,128]{3,1,2,0:T(8,128)(2,1)}, bf16[2,192,6,128]{3,1,2,0:T(8,128)(2,1)S(1)}, u32[]{:S(2)}, u32[]{:S(2)}) collective-permute-start(bf16[2,192,6,128]{3,1,2,0:T(8,128)(2,1)} %pad_maximum_fusion), channel_id=1, source_target_pairs={{12,0},{13,1},{14,2},{15,3},{28,16},{29,17},{30,18},{31,19}} | collective-permute-start | bytes 1769480 | tf_op jit(solution)/shard_map/ppermute | solution.py:18
  591.0 1.9 copy-start.6
  591.0 1.9 copy-start.15
  591.3 1.6 copy-start.7
  592.9 6.2 copy-start.1
  592.9 6.2 copy-start.2
  599.1 238.8 %copy-start.9 = (s32[5120]{0:T(1024)S(1)}, s32[5120]{0:T(1024)}, u32[]{:S(2)}) copy-start(s32[5120]{0:T(1024)} %param.25) | copy-start | bytes 61444
Sparse Core Ops, SparseCore 0:
  8.9 24.5 all-gather.4
  838.0 53.5 all-gather.6
